TPU v7x, 32 devices: a whole 2x2x4 slice. The times are simulated.
32 devices in a mesh: seq: 8 (over z, x), head: 4 (over y, core).
Axes of the slice: x: 2, y: 2, z: 4, core: 2. Of those that a mesh axis runs over, the one named last changes fastest.
Arguments:
- lin_query: bfloat16 [2048, 4096], P('seq', 'head'), may hold values from -2 to 2
- lin_key: bfloat16 [2048, 4096], P('seq', 'head'), may hold values from -2 to 2
- lin_value: bfloat16 [2048, 4096], P('seq', 'head'), may hold values from -130 to 130
- log_decay: float32 [2048, 32], P('seq', 'head'), may hold values from -2 to 0
- gate_logits: bfloat16 [2048, 4096], P('seq', 'head'), may hold values from -6 to 6
- norm_gain: float32 [4096], P('head'), may hold values from 0.25 to 1.75
- soft_query: bfloat16 [2048, 4096], P('seq', 'head'), may hold values from -4 to 4
- soft_key: bfloat16 [2048, 4096], P('seq', 'head'), may hold values from -4 to 4
- soft_value: bfloat16 [2048, 4096], P('seq', 'head'), may hold values from -6 to 6
- doc_ids: int32 [2048], P('seq'), may hold values from 0 to 8, as said below
- doc_spans: int32 [9, 2], replicated, may hold values from 0 to 2048, as said below
Outputs:
- lin_out: bfloat16 [2048, 4096], P('seq', 'head')
- soft_out: bfloat16 [2048, 4096], P('seq', 'head')
Inputs may be any that keep to these rules, and one draw needn't show every extreme that they name: `doc_ids`: never falls; document d covers exactly the positions doc_spans[d, 0] to doc_spans[d, 1] - 1. `doc_spans`: row 0 starts at 0, each row ends where the next starts, the last ends at 2048; every document holds 1 to 768 positions, and one holds exactly that many.
All inputs are finite; a program needn't handle non-finite values.
Results may differ from a plain program's by a relative error of at most 0.0053.
Values may be sent and summed in bfloat16 or wider, within the bound.
No kernel may reach another device: no remote copies, remote signals or barrier semaphores. Data moves between devices by JAX's collectives and lax.ppermute only.
A program may use at most 128 MiB of HBM per device.

v0:
```python
import jax
import jax.numpy as jnp
from jax import lax
from jax.sharding import PartitionSpec as P

HALF_MODEL_HEADS = 32
HD = 128
SPAN = 3


def entering(part, axis, combine, identity):
    place = lax.axis_index(axis)
    gathered = jax.tree.map(lambda a: lax.all_gather(a, axis), part)
    state = jax.tree.map(lambda a, e: jnp.zeros_like(a) + jnp.asarray(e, a.dtype), part, identity)

    def one(step, state):
        return combine(
            state, jax.tree.map(lambda a: lax.dynamic_index_in_dim(a, step, 0, False), gathered)
        )

    return lax.fori_loop(0, place, one, state)


def from_behind(array, axis, by):
    devices = lax.axis_size(axis)
    pairs = [(i, i + by) for i in range(devices) if 0 <= i + by < devices]
    return lax.ppermute(array, axis, pairs)


def combine(former, latter):
    return (former[0] * latter[0], latter[0][:, None, None] * former[1] + latter[1])


def shards(
    lin_query,
    lin_key,
    lin_value,
    log_decay,
    gate_logits,
    norm_gain,
    soft_query,
    soft_key,
    soft_value,
    doc_ids,
    doc_spans,
):
    token_rows = lin_query.shape[0]
    feature_width = lin_query.shape[1]
    head_count = feature_width // HD
    block_base = lax.axis_index("seq") * token_rows
    positions = block_base + jnp.arange(token_rows, dtype=jnp.int32)
    numbers = jnp.arange(doc_spans.shape[0], dtype=jnp.int32)
    starts = jnp.sum(
        jnp.where(doc_ids[:, None] == numbers[None, :], doc_spans[None, :, 0], 0), axis=1
    )
    queries = lin_query.reshape(token_rows, head_count, HD)
    key_rows = lin_key.reshape(token_rows, head_count, HD)
    value_rows = lin_value.reshape(token_rows, head_count, HD)
    cumulative = jnp.cumsum(log_decay, axis=0)
    scores = jnp.einsum("thd,shd->hts", queries, key_rows, preferred_element_type=jnp.float32)
    spread = cumulative.T[:, :, None] - cumulative.T[:, None, :]
    allowed = (positions[None, :] <= positions[:, None]) & (positions[None, :] >= starts[:, None])
    weights = jnp.where(allowed[None], scores * jnp.exp(jnp.minimum(spread, 0.0)), 0.0).astype(
        jnp.bfloat16
    )
    inner_part = jnp.einsum("hts,shd->thd", weights, value_rows, preferred_element_type=jnp.float32)
    last_cumul = cumulative[-1]
    tail_weight = jnp.where(
        (positions >= starts[-1])[:, None],
        jnp.exp(jnp.minimum(last_cumul[None, :] - cumulative, 0.0)),
        0.0,
    )
    tail_key = (key_rows.astype(jnp.float32) * tail_weight[:, :, None]).astype(jnp.bfloat16)
    local_state = jnp.einsum(
        "shd,she->hde", tail_key, value_rows, preferred_element_type=jnp.float32
    )
    local_decay = jnp.where(starts[-1] < block_base, jnp.exp(last_cumul), 0.0)
    entry_scale = jnp.where((starts < block_base)[:, None], jnp.exp(cumulative), 0.0)
    identity = (jnp.ones_like(local_decay), jnp.zeros_like(local_state))
    carried = entering((local_decay, local_state), "seq", combine, identity)[1]
    cross_part = (
        jnp.einsum(
            "thd,hde->the",
            queries,
            carried.astype(jnp.bfloat16),
            preferred_element_type=jnp.float32,
        )
        * entry_scale[:, :, None]
    )
    mixture = inner_part + cross_part
    squares = jnp.sum(mixture * mixture, axis=(1, 2))
    norm_total = lax.psum(squares, "head")
    norm_scale = lax.rsqrt(norm_total / (HALF_MODEL_HEADS * HD) + 1e-06)
    lin_out = (
        mixture.reshape(token_rows, feature_width)
        * norm_scale[:, None]
        * norm_gain[None, :]
        * jax.nn.sigmoid(gate_logits.astype(jnp.float32))
    ).astype(jnp.bfloat16)
    key_parts = [soft_key]
    value_parts = [soft_value]
    for distance in range(1, SPAN + 1):
        earlier = from_behind((soft_key, soft_value), "seq", distance)
        key_parts.insert(0, earlier[0])
        value_parts.insert(0, earlier[1])
    all_keys = jnp.concatenate(key_parts, axis=0)
    all_values = jnp.concatenate(value_parts, axis=0)
    span_rows = all_keys.shape[0]
    key_pos = block_base + token_rows - span_rows + jnp.arange(span_rows, dtype=jnp.int32)
    soft_queries = soft_query.reshape(token_rows, head_count, HD)
    logits = jnp.einsum(
        "thd,shd->hts",
        soft_queries,
        all_keys.reshape(span_rows, head_count, HD),
        preferred_element_type=jnp.float32,
    ) * HD ** (-0.5)
    visible = (key_pos[None, :] >= starts[:, None]) & (key_pos[None, :] <= positions[:, None])
    logits = jnp.where(visible[None], logits, -jnp.inf)
    row_max = jnp.max(logits, axis=2, keepdims=True)
    soft_weights = jnp.exp(logits - row_max)
    soft_total = jnp.sum(soft_weights, axis=2)
    attended = jnp.einsum(
        "hts,shd->thd",
        soft_weights.astype(jnp.bfloat16),
        all_values.reshape(span_rows, head_count, HD),
        preferred_element_type=jnp.float32,
    )
    soft_out = (
        (attended / soft_total.T[:, :, None])
        .reshape(token_rows, feature_width)
        .astype(jnp.bfloat16)
    )
    return (lin_out, soft_out)


def solution(mesh):
    in_specs = (
        P("seq", "head"),
        P("seq", "head"),
        P("seq", "head"),
        P("seq", "head"),
        P("seq", "head"),
        P("head"),
        P("seq", "head"),
        P("seq", "head"),
        P("seq", "head"),
        P("seq"),
        P(),
    )
    out_specs = (P("seq", "head"), P("seq", "head"))
    return jax.shard_map(shards, mesh=mesh, in_specs=in_specs, out_specs=out_specs, check_vma=False)
```

profile of v0, /device:TPU:30, one launch (start us, length us, event | category | flops | bytes accessed | tf_op | source)
XLA Modules:
  0.0 212.4 jit_solution(500775631223508674)
XLA Ops:
  10.7 1.3 reduce-window.6
  12.1 1.2 copy.96
  13.7 2.1 %fusion.22 = f32[8,128,128]{2,1,0:T(8,128)} fusion(bf16[256,8,128]{0,2,1:T(8,128)(2,1)S(1)} %bitcast.97, f32[256,8]{0,1:T(8,128)S(1)} %exponential_select_fusion.1, bf16[256,1024]{1,0:T(8,128)(2,1)} %param.15), kind=kOutput, calls=%fused_computation.30 | convolution fusion | flops 67895296 | bytes 1581056 | tf_op jit(solution)/shard_map/shd,she->hde/dot_general | solution.py:74
  15.9 2.1 copy.85
  17.9 1.3 collective-permute-start.3
  19.2 1.3 collective-permute-start.4
  20.5 1.3 collective-permute-start
  21.8 1.3 collective-permute-start.1
  23.1 1.3 collective-permute-start.2
  24.4 136.3 %all-gather.1 = f32[8,1,8]{2,1,0:T(1,128)S(1)} all-gather(f32[1,1,8]{2,1,0:T(1,128)S(1)} %bitcast.106), channel_id=1, replica_groups=mesh['seq'=8,'head'=4] {'seq'}, dimensions={0}, use_global_device_ids=true | all-gather | bytes 288 | tf_op jit(solution)/shard_map/all_gather | solution.py:13
  160.9 1.3 collective-permute-start.5
  163.3 1.7 pad_maximum_fusion
  165.0 2.6 %copy.84 = bf16[1024,1024]{0,1:T(8,128)(2,1)} copy(bf16[1024,1024]{1,0:T(8,128)(2,1)S(1)} %pad_maximum_fusion) | data formatting | bytes 4194304 | tf_op jit(solution)/shard_map/concatenate | solution.py:107
  167.6 6.7 %collective-permute-done.5 = bf16[256,1024]{0,1:T(8,128)(2,1)} collective-permute-done((bf16[256,1024]{0,1:T(8,128)(2,1)}, bf16[256,1024]{0,1:T(8,128)(2,1)}, u32[]{:S(2)}, u32[]{:S(2)}) %collective-permute-start.5) | collective-permute-done | bytes 524320 | tf_op jit(solution)/shard_map/ppermute | solution.py:27
  174.4 1.8 pad_maximum_fusion.1
  176.2 1.7 fusion.2
  177.9 1.7 fusion
  179.6 2.2 %divide_convert_fusion = bf16[256,8,128]{0,2,1:T(8,128)(2,1)S(1)} fusion(bf16[1024,8,128]{0,2,1:T(8,128)(2,1)S(1)} %bitcast.99, f32[8,1024,256]{2,1,0:T(8,128)S(1)} %get-tuple-element.74, f32[8,256]{1,0:T(8,128)S(1)} %get-tuple-element.73, pred[256,1024]{0,1:T(8,128)(4,1)S(1)} %compare_and_fusion, f32[256,8]{0,1:T(8,128)S(1)} %bitcast.104), kind=kOutput, calls=%fused_computation.21 | convolution fusion | flops 545783808 | bytes 11288576 | tf_op jit(solution)/shard_map/hts,shd->thd/dot_general | solution.py:122
  181.8 1.0 copy.92
  182.9 8.7 %while.12 = (s32[]{:T(128)}, f32[8,128,128]{2,1,0:T(8,128)S(1)}, s32[]{:T(128)}, f32[8,8]{1,0:T(8,128)S(1)}, f32[8,8,128,128]{3,2,1,0:T(8,128)}, /*index=5*/s32[]{:T(128)}, s32[]{:T(128)}, s32[]{:T(128)}) while((s32[]{:T(128)}, f32[8,128,128]{2,1,0:T(8,128)S(1)}, s32[]{:T(128)}, f32[8,8]{1,0:T(8,128)S(1)}, f32[8,8,128,128]{3,2,1,0:T(8,128)}, ...), condition=%wide.region_4.5_spmd, body=%wide.region_3.4_spmd.sunk | while | flops 262149 | bytes 1573087 | solution.py:21
  182.9 1.2 bitcast_add_fusion.2
  184.2 1.2 bitcast_add_fusion.2
  185.4 1.2 bitcast_add_fusion.2
  186.7 1.2 bitcast_add_fusion.2
  187.9 1.2 bitcast_add_fusion.2
  189.1 1.2 bitcast_add_fusion.2
  190.4 1.2 bitcast_add_fusion.2
  191.6 1.4 fusion.12
  193.0 2.9 %multiply_reduce_fusion = (f32[256]{0:T(256)S(1)}, f32[256,8,128]{0,2,1:T(8,128)}) fusion(f32[256,8,128]{0,2,1:T(8,128)S(1)} %fusion.12, bf16[256,8,128]{0,2,1:T(8,128)(2,1)S(1)} %bitcast.98, f32[8,256]{1,0:T(8,128)S(1)} %add_bitcast_fusion.1, pred[256,256]{1,0:T(8,128)(4,1)S(1)} %compare_and_fusion.1, bf16[256,1024]{1,0:T(8,128)(2,1)S(1)} %copy-done.2, ...), kind=kOutput, calls=%fused_computation.23 | convolution fusion | flops 271843072 | bytes 3744768 | tf_op jit(solution)/shard_map/hts,shd->thd/dot_general | solution.py:66
  195.9 1.6 copy.83
  197.5 5.9 %psum.7 = f32[256]{0:T(256)S(1)} all-reduce(f32[256]{0:T(256)S(1)} %get-tuple-element.71), channel_id=1, replica_groups=mesh['seq'=8,'head'=4] {'head'}, use_global_device_ids=true, to_apply=%region_6.7 | all-reduce | flops 256 | bytes 2048 | tf_op jit(solution)/shard_map/psum | solution.py:92
  203.4 2.2 %multiply_convert_fusion = bf16[256,1024]{1,0:T(8,128)(2,1)} fusion(bf16[256,1024]{1,0:T(8,128)(2,1)} %param.17, f32[256,1024]{1,0:T(8,128)S(1)} %copy.83, f32[1024]{0:T(1024)S(1)} %copy-done.6, f32[256]{0:T(256)S(1)} %add_rsqrt_fusion), kind=kLoop, calls=%fused_computation.22 | loop fusion | flops 2097152 | bytes 2102272 | tf_op jit(solution)/shard_map/convert_element_type | solution.py:99
  (46 shorter events, 4.8 us)
Async XLA Ops:
  7.2 169.0 %copy-start = (bf16[256,1024]{1,0:T(8,128)(2,1)S(1)}, bf16[256,1024]{1,0:T(8,128)(2,1)}, u32[]{:S(2)}) copy-start(bf16[256,1024]{1,0:T(8,128)(2,1)} %param.19) | copy-start | bytes 1572868
  7.2 13.3 %copy-start.3 = (bf16[256,1024]{1,0:T(8,128)(2,1)S(1)}, bf16[256,1024]{1,0:T(8,128)(2,1)}, u32[]{:S(2)}) copy-start(bf16[256,1024]{1,0:T(8,128)(2,1)} %param.21) | copy-start | bytes 1572868
  7.2 175.6 %all-gather.4.cloned.1.call-start = ((), (), s32[]{:S(2)}) async-start(), calls=%async_computation | async-start | bytes 4718592 | tf_op jit(solution)/shard_map/all_gather | solution.py:13
  17.9 149.7 %collective-permute-start.3 = (bf16[256,1024]{0,1:T(8,128)(2,1)}, bf16[256,1024]{0,1:T(8,128)(2,1)}, u32[]{:S(2)}, u32[]{:S(2)}) collective-permute-start(bf16[256,1024]{0,1:T(8,128)(2,1)} %copy.85), channel_id=1, source_target_pairs={{0,12},{4,16},{8,20},{12,24},{16,28},{1,13},{5,17},{9,21},{13,25},... | collective-permute-start | bytes 1572872 | tf_op jit(solution)/shard_map/ppermute | solution.py:27
  19.2 148.4 %collective-permute-start.4 = (bf16[256,1024]{0,1:T(8,128)(2,1)}, bf16[256,1024]{0,1:T(8,128)(2,1)}, u32[]{:S(2)}, u32[]{:S(2)}) collective-permute-start(bf16[256,1024]{0,1:T(8,128)(2,1)} %copy.85), channel_id=1, source_target_pairs={{0,8},{4,12},{8,16},{12,20},{16,24},{20,28},{1,9},{5,13},{9,17},{1... | collective-permute-start | bytes 1572872 | tf_op jit(solution)/shard_map/ppermute | solution.py:27
  20.5 140.4 %collective-permute-start = (bf16[256,1024]{1,0:T(8,128)(2,1)S(1)}, bf16[256,1024]{1,0:T(8,128)(2,1)S(1)}, u32[]{:S(2)}, u32[]{:S(2)}) collective-permute-start(bf16[256,1024]{1,0:T(8,128)(2,1)S(1)} %copy-done.3), channel_id=1, source_target_pairs={{0,12},{4,16},{8,20},{12,24},{16,28},{1,13},{5,17},{9,21},{13,25},... | collective-permute-start | bytes 1572872 | tf_op jit(solution)/shard_map/ppermute | solution.py:27
  21.8 140.7 %collective-permute-start.1 = (bf16[256,1024]{1,0:T(8,128)(2,1)S(1)}, bf16[256,1024]{1,0:T(8,128)(2,1)S(1)}, u32[]{:S(2)}, u32[]{:S(2)}) collective-permute-start(bf16[256,1024]{1,0:T(8,128)(2,1)S(1)} %copy-done.3), channel_id=1, source_target_pairs={{0,8},{4,12},{8,16},{12,20},{16,24},{20,28},{1,9},{5,13},{9,17},{1... | collective-permute-start | bytes 1572872 | tf_op jit(solution)/shard_map/ppermute | solution.py:27
  23.1 140.2 %collective-permute-start.2 = (bf16[256,1024]{1,0:T(8,128)(2,1)S(1)}, bf16[256,1024]{1,0:T(8,128)(2,1)}, u32[]{:S(2)}, u32[]{:S(2)}) collective-permute-start(bf16[256,1024]{1,0:T(8,128)(2,1)S(1)} %copy-done.3), channel_id=1, source_target_pairs={{0,4},{4,8},{8,12},{12,16},{16,20},{20,24},{24,28},{1,5},{5,9},{9,... | collective-permute-start | bytes 1572872 | tf_op jit(solution)/shard_map/ppermute | solution.py:27
  160.9 1.6 copy-start.4
  160.9 13.4 %collective-permute-start.5 = (bf16[256,1024]{0,1:T(8,128)(2,1)}, bf16[256,1024]{0,1:T(8,128)(2,1)}, u32[]{:S(2)}, u32[]{:S(2)}) collective-permute-start(bf16[256,1024]{0,1:T(8,128)(2,1)} %copy.85), channel_id=1, source_target_pairs={{0,4},{4,8},{8,12},{12,16},{16,20},{20,24},{24,28},{1,5},{5,9},{9,... | collective-permute-start | bytes 1572872 | tf_op jit(solution)/shard_map/ppermute | solution.py:27
  162.5 0.8 copy-start.5
  177.9 1.7 copy-start.1
  182.9 10.1 %copy-start.2 = (bf16[256,1024]{1,0:T(8,128)(2,1)S(1)}, bf16[256,1024]{1,0:T(8,128)(2,1)}, u32[]{:S(2)}) copy-start(bf16[256,1024]{1,0:T(8,128)(2,1)} %param.15) | copy-start | bytes 1572868
  193.0 10.4 %copy-start.6 = (f32[1024]{0:T(1024)S(1)}, f32[1024]{0:T(1024)}, u32[]{:S(2)}) copy-start(f32[1024]{0:T(1024)} %param.18) | copy-start | bytes 12292
Sparse Core Ops, SparseCore 0:
  16.0 114.9 all-gather.3
where the time goes:
time: 213 us; the launch traced here: 212 us
  blocking collectives  142 us (67%)
  other arithmetic  19.3 us (9%)
  between operations  14.9 us (7%)
  local copies, waits for them, and re-layouts  10.9 us (5%)
  matrix products  10.4 us (5%)
  starting transfers between devices  7.77 us (4%)
  waiting for transfers between devices  6.78 us (3%)
    all_gather x1, blocking collectives, entering(): gathered = jax.tree.map(lambda a: lax.all_gather(a, axis), part)  136 us
    add x7, other arithmetic, combine(): latter[0][:, None, None] * former[1] + latter[1]  8.38 us
    ppermute x6, starting transfers between devices, from_behind(): return lax.ppermute(array, axis, pairs)  7.73 us
    ppermute x6, waiting for transfers between devices, from_behind(): return lax.ppermute(array, axis, pairs)  6.76 us
    psum x1, blocking collectives, shards(): norm_total = lax.psum(squares, 'head')  5.89 us
  transfers between devices with their start and end apart: 7, of which 1 were waited for; matrix products, arithmetic and copies ran while one was open for 7% of the time, Pallas kernels for 0%

commit v1 on v0

--- a/solution.py
+++ b/solution.py
@@ -89,7 +89,7 @@
     )
     mixture = inner_part + cross_part
     squares = jnp.sum(mixture * mixture, axis=(1, 2))
-    norm_total = lax.psum(squares, "head")
+    norm_total = jnp.sum(lax.all_gather(squares, "head"), axis=0)
     norm_scale = lax.rsqrt(norm_total / (HALF_MODEL_HEADS * HD) + 1e-06)
     lin_out = (
         mixture.reshape(token_rows, feature_width)

time: 213 us -> 213 us (level)
    psum x1 -> x0, blocking collectives: 5.89 us -> none  [shards(): norm_total = lax.psum(squares, 'head')]
    all_gather x0 -> x1, blocking collectives: none -> 5.07 us  [shards(): norm_total = jnp.sum(lax.all_gather(squares, 'head'), axis=0)]
where the time goes in v1:
time: 213 us; the launch traced here: 212 us
  blocking collectives  141 us (66%)
  other arithmetic  19.3 us (9%)
  between operations  14.9 us (7%)
  local copies, waits for them, and re-layouts  10.9 us (5%)
  matrix products  10.4 us (5%)
  starting transfers between devices  7.77 us (4%)
  waiting for transfers between devices  6.78 us (3%)
    all_gather x1, blocking collectives, entering(): gathered = jax.tree.map(lambda a: lax.all_gather(a, axis), part)  136 us
    add x7, other arithmetic, combine(): latter[0][:, None, None] * former[1] + latter[1]  8.38 us
    ppermute x6, starting transfers between devices, from_behind(): return lax.ppermute(array, axis, pairs)  7.73 us
    ppermute x6, waiting for transfers between devices, from_behind(): return lax.ppermute(array, axis, pairs)  6.76 us
    all_gather x1, blocking collectives, shards(): norm_total = jnp.sum(lax.all_gather(squares, 'head'), axis=0)  5.07 us
  transfers between devices with their start and end apart: 7, of which 1 were waited for; matrix products, arithmetic and copies ran while one was open for 7% of the time, Pallas kernels for 0%

profile of v1, /device:TPU:30, one launch (start us, length us, event | category | flops | bytes accessed | tf_op | source)
XLA Modules:
  0.0 211.6 jit_solution(15708293584865546018)
XLA Ops:
  10.7 1.3 reduce-window.6
  12.1 1.2 copy.96
  13.7 2.1 %fusion.22 = f32[8,128,128]{2,1,0:T(8,128)} fusion(bf16[256,8,128]{0,2,1:T(8,128)(2,1)S(1)} %bitcast.98, f32[256,8]{0,1:T(8,128)S(1)} %exponential_select_fusion.1, bf16[256,1024]{1,0:T(8,128)(2,1)} %param.15), kind=kOutput, calls=%fused_computation.30 | convolution fusion | flops 67895296 | bytes 1581056 | tf_op jit(solution)/shard_map/shd,she->hde/dot_general | solution.py:74
  15.9 2.1 copy.85
  17.9 1.3 collective-permute-start.3
  19.2 1.3 collective-permute-start.4
  20.5 1.3 collective-permute-start
  21.8 1.3 collective-permute-start.1
  23.1 1.3 collective-permute-start.2
  24.4 136.3 %all-gather.2 = f32[8,1,8]{2,1,0:T(1,128)S(1)} all-gather(f32[1,1,8]{2,1,0:T(1,128)S(1)} %bitcast.107), channel_id=1, replica_groups=mesh['seq'=8,'head'=4] {'seq'}, dimensions={0}, use_global_device_ids=true | all-gather | bytes 288 | tf_op jit(solution)/shard_map/all_gather | solution.py:13
  160.9 1.3 collective-permute-start.5
  163.3 1.7 pad_maximum_fusion
  165.0 2.6 %copy.84 = bf16[1024,1024]{0,1:T(8,128)(2,1)} copy(bf16[1024,1024]{1,0:T(8,128)(2,1)S(1)} %pad_maximum_fusion) | data formatting | bytes 4194304 | tf_op jit(solution)/shard_map/concatenate | solution.py:107
  167.6 6.7 %collective-permute-done.5 = bf16[256,1024]{0,1:T(8,128)(2,1)} collective-permute-done((bf16[256,1024]{0,1:T(8,128)(2,1)}, bf16[256,1024]{0,1:T(8,128)(2,1)}, u32[]{:S(2)}, u32[]{:S(2)}) %collective-permute-start.5) | collective-permute-done | bytes 524320 | tf_op jit(solution)/shard_map/ppermute | solution.py:27
  174.4 1.8 pad_maximum_fusion.1
  176.2 1.7 fusion.2
  177.9 1.7 fusion
  179.6 2.2 %divide_convert_fusion = bf16[256,8,128]{0,2,1:T(8,128)(2,1)S(1)} fusion(bf16[1024,8,128]{0,2,1:T(8,128)(2,1)S(1)} %bitcast.100, f32[8,1024,256]{2,1,0:T(8,128)S(1)} %get-tuple-element.74, f32[8,256]{1,0:T(8,128)S(1)} %get-tuple-element.73, pred[256,1024]{0,1:T(8,128)(4,1)S(1)} %compare_and_fusion, f32[256,8]{0,1:T(8,128)S(1)} %bitcast.105), kind=kOutput, calls=%fused_computation.21 | convolution fusion | flops 545783808 | bytes 11288576 | tf_op jit(solution)/shard_map/hts,shd->thd/dot_general | solution.py:122
  181.8 1.0 copy.92
  182.9 8.7 %while.12 = (s32[]{:T(128)}, f32[8,128,128]{2,1,0:T(8,128)S(1)}, s32[]{:T(128)}, f32[8,8]{1,0:T(8,128)S(1)}, f32[8,8,128,128]{3,2,1,0:T(8,128)}, /*index=5*/s32[]{:T(128)}, s32[]{:T(128)}, s32[]{:T(128)}) while((s32[]{:T(128)}, f32[8,128,128]{2,1,0:T(8,128)S(1)}, s32[]{:T(128)}, f32[8,8]{1,0:T(8,128)S(1)}, f32[8,8,128,128]{3,2,1,0:T(8,128)}, ...), condition=%wide.region_4.5_spmd, body=%wide.region_3.4_spmd.sunk | while | flops 262149 | bytes 1573087 | solution.py:21
  182.9 1.2 bitcast_add_fusion.2
  184.2 1.2 bitcast_add_fusion.2
  185.4 1.2 bitcast_add_fusion.2
  186.7 1.2 bitcast_add_fusion.2
  187.9 1.2 bitcast_add_fusion.2
  189.1 1.2 bitcast_add_fusion.2
  190.4 1.2 bitcast_add_fusion.2
  191.6 1.4 fusion.12
  193.0 2.9 %multiply_reduce_fusion = (f32[256]{0:T(256)S(1)}, f32[256,8,128]{0,2,1:T(8,128)}) fusion(f32[256,8,128]{0,2,1:T(8,128)S(1)} %fusion.12, bf16[256,8,128]{0,2,1:T(8,128)(2,1)S(1)} %bitcast.99, f32[8,256]{1,0:T(8,128)S(1)} %add_bitcast_fusion.1, pred[256,256]{1,0:T(8,128)(4,1)S(1)} %compare_and_fusion.1, bf16[256,1024]{1,0:T(8,128)(2,1)S(1)} %copy-done.2, ...), kind=kOutput, calls=%fused_computation.23 | convolution fusion | flops 271843072 | bytes 3744768 | tf_op jit(solution)/shard_map/hts,shd->thd/dot_general | solution.py:66
  195.9 1.6 copy.83
  197.5 5.1 %all-gather.3 = f32[4,1,256]{2,1,0:T(1,128)S(1)} all-gather(f32[1,1,256]{2,1,0:T(1,128)S(1)} %bitcast.108), channel_id=3, replica_groups=mesh['seq'=8,'head'=4] {'head'}, dimensions={0}, use_global_device_ids=true | all-gather | bytes 5120 | tf_op jit(solution)/shard_map/all_gather | solution.py:92
  202.6 2.2 %multiply_convert_fusion = bf16[256,1024]{1,0:T(8,128)(2,1)} fusion(bf16[256,1024]{1,0:T(8,128)(2,1)} %param.17, f32[256,1024]{1,0:T(8,128)S(1)} %copy.83, f32[1024]{0:T(1024)S(1)} %copy-done.6, f32[256]{0:T(256)S(1)} %add_rsqrt_fusion), kind=kLoop, calls=%fused_computation.22 | loop fusion | flops 2097152 | bytes 2102272 | tf_op jit(solution)/shard_map/convert_element_type | solution.py:99
  (47 shorter events, 4.8 us)
Async XLA Ops:
  7.2 169.0 %copy-start = (bf16[256,1024]{1,0:T(8,128)(2,1)S(1)}, bf16[256,1024]{1,0:T(8,128)(2,1)}, u32[]{:S(2)}) copy-start(bf16[256,1024]{1,0:T(8,128)(2,1)} %param.19) | copy-start | bytes 1572868
  7.2 13.3 %copy-start.3 = (bf16[256,1024]{1,0:T(8,128)(2,1)S(1)}, bf16[256,1024]{1,0:T(8,128)(2,1)}, u32[]{:S(2)}) copy-start(bf16[256,1024]{1,0:T(8,128)(2,1)} %param.21) | copy-start | bytes 1572868
  7.2 175.6 %all-gather.6.cloned.1.call-start = ((), (), s32[]{:S(2)}) async-start(), calls=%async_computation | async-start | bytes 4718592 | tf_op jit(solution)/shard_map/all_gather | solution.py:13
  17.9 149.7 %collective-permute-start.3 = (bf16[256,1024]{0,1:T(8,128)(2,1)}, bf16[256,1024]{0,1:T(8,128)(2,1)}, u32[]{:S(2)}, u32[]{:S(2)}) collective-permute-start(bf16[256,1024]{0,1:T(8,128)(2,1)} %copy.85), channel_id=1, source_target_pairs={{0,12},{4,16},{8,20},{12,24},{16,28},{1,13},{5,17},{9,21},{13,25},... | collective-permute-start | bytes 1572872 | tf_op jit(solution)/shard_map/ppermute | solution.py:27
  19.2 148.4 %collective-permute-start.4 = (bf16[256,1024]{0,1:T(8,128)(2,1)}, bf16[256,1024]{0,1:T(8,128)(2,1)}, u32[]{:S(2)}, u32[]{:S(2)}) collective-permute-start(bf16[256,1024]{0,1:T(8,128)(2,1)} %copy.85), channel_id=1, source_target_pairs={{0,8},{4,12},{8,16},{12,20},{16,24},{20,28},{1,9},{5,13},{9,17},{1... | collective-permute-start | bytes 1572872 | tf_op jit(solution)/shard_map/ppermute | solution.py:27
  20.5 140.4 %collective-permute-start = (bf16[256,1024]{1,0:T(8,128)(2,1)S(1)}, bf16[256,1024]{1,0:T(8,128)(2,1)S(1)}, u32[]{:S(2)}, u32[]{:S(2)}) collective-permute-start(bf16[256,1024]{1,0:T(8,128)(2,1)S(1)} %copy-done.3), channel_id=1, source_target_pairs={{0,12},{4,16},{8,20},{12,24},{16,28},{1,13},{5,17},{9,21},{13,25},... | collective-permute-start | bytes 1572872 | tf_op jit(solution)/shard_map/ppermute | solution.py:27
  21.8 140.7 %collective-permute-start.1 = (bf16[256,1024]{1,0:T(8,128)(2,1)S(1)}, bf16[256,1024]{1,0:T(8,128)(2,1)S(1)}, u32[]{:S(2)}, u32[]{:S(2)}) collective-permute-start(bf16[256,1024]{1,0:T(8,128)(2,1)S(1)} %copy-done.3), channel_id=1, source_target_pairs={{0,8},{4,12},{8,16},{12,20},{16,24},{20,28},{1,9},{5,13},{9,17},{1... | collective-permute-start | bytes 1572872 | tf_op jit(solution)/shard_map/ppermute | solution.py:27
  23.1 140.2 %collective-permute-start.2 = (bf16[256,1024]{1,0:T(8,128)(2,1)S(1)}, bf16[256,1024]{1,0:T(8,128)(2,1)}, u32[]{:S(2)}, u32[]{:S(2)}) collective-permute-start(bf16[256,1024]{1,0:T(8,128)(2,1)S(1)} %copy-done.3), channel_id=1, source_target_pairs={{0,4},{4,8},{8,12},{12,16},{16,20},{20,24},{24,28},{1,5},{5,9},{9,... | collective-permute-start | bytes 1572872 | tf_op jit(solution)/shard_map/ppermute | solution.py:27
  160.9 1.6 copy-start.4
  160.9 13.4 %collective-permute-start.5 = (bf16[256,1024]{0,1:T(8,128)(2,1)}, bf16[256,1024]{0,1:T(8,128)(2,1)}, u32[]{:S(2)}, u32[]{:S(2)}) collective-permute-start(bf16[256,1024]{0,1:T(8,128)(2,1)} %copy.85), channel_id=1, source_target_pairs={{0,4},{4,8},{8,12},{12,16},{16,20},{20,24},{24,28},{1,5},{5,9},{9,... | collective-permute-start | bytes 1572872 | tf_op jit(solution)/shard_map/ppermute | solution.py:27
  162.5 0.8 copy-start.5
  177.9 1.7 copy-start.1
  182.9 10.1 %copy-start.2 = (bf16[256,1024]{1,0:T(8,128)(2,1)S(1)}, bf16[256,1024]{1,0:T(8,128)(2,1)}, u32[]{:S(2)}) copy-start(bf16[256,1024]{1,0:T(8,128)(2,1)} %param.15) | copy-start | bytes 1572868
  193.0 9.6 %copy-start.6 = (f32[1024]{0:T(1024)S(1)}, f32[1024]{0:T(1024)}, u32[]{:S(2)}) copy-start(f32[1024]{0:T(1024)} %param.18) | copy-start | bytes 12292
Sparse Core Ops, SparseCore 0:
  16.0 114.9 all-gather.5
